TPU v7x, 256 devices: a whole 4x4x8 slice. The times are simulated.
256 devices in a mesh: dp: 64 (over z, y, core), mp: 4 (over x).
Axes of the slice: x: 4, y: 4, z: 8, core: 2. Of those that a mesh axis runs over, the one named last changes fastest.
Arguments:
- tokens: bfloat16 [49152, 768], P(('dp', 'mp')), may hold values from -6 to 6
- obs_mask: int32 [768, 64], P(('dp', 'mp')), may hold values 0 or 1
- norm_gains: float32 [5, 768], replicated, may hold values from 0.1 to 1.9
- attn_in: bfloat16 [2, 3, 768, 768], P(None, None, 'dp', 'mp'), may hold values from -0.21875 to 0.21875
- attn_out: bfloat16 [2, 768, 768], P(None, 'mp', 'dp'), may hold values from -0.21875 to 0.21875
- mlp_in: bfloat16 [2, 768, 3072], P(None, 'dp', 'mp'), may hold values from -0.21875 to 0.21875
- mlp_out: bfloat16 [2, 3072, 768], P(None, 'mp', 'dp'), may hold values from -0.109375 to 0.109375
- embodiment: int32 [768, 1], P('dp'), may hold values from 0 to 24; in each aligned block of 12 rows (0 to 11, 12 to 23, ...) no two rows name the same one
- levels: int32 [768, 2], P('dp'), may hold values from 0 to 19
- actions: bfloat16 [768, 2, 56], P('dp'), may hold values from -1 to 1
- noise: bfloat16 [768, 2, 56], P('dp'), may hold values from -5 to 5
- action_dims: int32 [25], replicated, may hold values from 7 to 14
- head_read: bfloat16 [64, 768, 256], P('dp'), may hold values from -0.21875 to 0.21875
- head_act: bfloat16 [64, 56, 256], P('dp'), may hold values from -0.75 to 0.75
- time_table: bfloat16 [64, 20, 256], P('dp'), may hold values from -5 to 5
- block_in: bfloat16 [64, 256, 256], P('dp'), may hold values from -0.375 to 0.375
- block_out: bfloat16 [64, 256, 256], P('dp'), may hold values from -0.375 to 0.375
- head_out: bfloat16 [64, 256, 56], P('dp'), may hold values from -0.375 to 0.375
Outputs:
- readout_grad: bfloat16 [768, 2, 768], P(('dp', 'mp'))
- grad_read: float32 [64, 768, 256], P('dp', 'mp')
- grad_act: float32 [64, 56, 256], P('dp')
- grad_time: float32 [64, 20, 256], P('dp')
- grad_block_in: float32 [64, 256, 256], P('dp')
- grad_block_out: float32 [64, 256, 256], P('dp')
- grad_head_out: float32 [64, 256, 56], P('dp')
Inputs may be any that keep to these rules, and one draw needn't show every extreme that they name: Within each aligned block of 12 samples (those of one dp index) no embodiment appears twice; every embodiment appears in some block.
All inputs are finite; a program needn't handle non-finite values. No bound on the sum of `obs_mask` on one device may be relied on, other than what follows from the above.
Results may differ from a plain program's by a relative error of at most 0.024.
Values may be sent and summed in bfloat16 or wider, within the bound.
No kernel may reach another device: no remote copies, remote signals or barrier semaphores. Data moves between devices by JAX's collectives and lax.ppermute only.
A program may use at most 64 MiB of HBM per device.

v0:
```python
import math
import jax
import jax.numpy as jnp
from jax import lax
from jax.sharding import Mesh, PartitionSpec as P

D = 768
HDIM = 64
EMB = 25
READ = 2
LEVELS = 20
ADIM_MAX = 14
ACT = 56
SEQ = 64
F32 = jnp.float32
BF16 = jnp.bfloat16
DP = ("z", "y", "c")
norm_eps = 1e-05


def sent_to_all(x, axis):
    copies = jnp.broadcast_to(x, (lax.axis_size(axis), *x.shape))
    return lax.all_to_all(copies, axis, split_axis=0, concat_axis=0, tiled=True)


def gather_rows(x, axis):
    pieces = sent_to_all(x, axis)
    return pieces.reshape(-1, *x.shape[1:])


def summed_on_arrival(x, axis):
    pieces = x.reshape(lax.axis_size(axis), -1, x.shape[1])
    arrived = lax.all_to_all(pieces, axis, split_axis=0, concat_axis=0, tiled=True)
    return arrived.astype(F32).sum(axis=0)


def summed_for_all(x, axis):
    return sent_to_all(x, axis).astype(F32).sum(axis=0)


def gather_turned(arrays, axis, dims):
    turned = [jnp.moveaxis(a, dim, 0) for a, dim in zip(arrays, dims)]
    widths = [t[0].size for t in turned]
    both = jnp.concatenate([t.reshape(-1, w) for t, w in zip(turned, widths)], axis=1)
    whole = lax.all_gather(both, axis, axis=0, tiled=True)
    pieces = jnp.split(whole, [sum(widths[:k]) for k in range(1, len(widths))], axis=1)
    return tuple(
        (
            jnp.moveaxis(b.reshape(-1, *t.shape[1:]), 0, dim)
            for b, t, dim in zip(pieces, turned, dims)
        )
    )


def normalize(values, scale_gain):
    center = values - jnp.mean(values, axis=-1, keepdims=True)
    spread = jnp.mean(center * center, axis=-1, keepdims=True)
    return center * lax.rsqrt(spread + norm_eps) * scale_gain


def mm(a, b):
    return jnp.dot(a, b, preferred_element_type=F32)


def allowed_keys(observed):
    length = observed.shape[1]
    position = jnp.arange(length)
    visible = (observed == 1) & (position < length - READ)[None, :]
    itself = position[:, None] == position[None, :]
    return visible[:, None, :] | itself[None, :, :]


def attend(queries, key_rows, value_rows, allowed):
    scores = jnp.einsum(
        "sqhd,skhd->shqk", queries, key_rows, preferred_element_type=F32
    ) * HDIM ** (-0.5)
    weights = jnp.where(allowed[:, None, :, :], jnp.exp(scores), 0.0)
    shares = (weights / jnp.sum(weights, axis=-1, keepdims=True)).astype(BF16)
    context = jnp.einsum("shqk,skhd->sqhd", shares, value_rows, preferred_element_type=F32)
    return context.astype(BF16)


def plan():
    steps_up = (jnp.arange(LEVELS, dtype=F32) + 1.0) / LEVELS
    anchor = math.cos(0.008 / 1.008 * math.pi / 2) ** 2
    return jnp.cos((steps_up + 0.008) / 1.008 * (math.pi / 2)) ** 2 / anchor


def noisy_pair(level_ids, clean, noise_draw, table):
    picked = (level_ids[..., None] == jnp.arange(LEVELS)).astype(F32)
    kept = jnp.sum(picked * table, axis=-1)[..., None]
    mixed = jnp.sqrt(kept) * clean.astype(F32) + jnp.sqrt(1.0 - kept) * noise_draw.astype(F32)
    return mixed.astype(BF16)


def tail(first, target, weight_mask, inner_weight, outer_weight, final_weight):
    active = jax.nn.silu(first).astype(BF16)
    inner = jnp.dot(active, inner_weight, preferred_element_type=F32)
    second = jax.nn.silu(inner).astype(BF16)
    hidden = first + jnp.dot(second, outer_weight, preferred_element_type=F32)
    third = jax.nn.silu(hidden).astype(BF16)
    predicted = jnp.dot(third, final_weight, preferred_element_type=F32)
    differ = predicted - target
    return 0.5 * jnp.sum(weight_mask * differ * differ)


def head_grads(first, inner_weight, outer_weight, final_weight, target, weight_mask):

    def head_loss(first_in, inner_in, outer_in, final_in):
        return tail(first_in, target, weight_mask, inner_in, outer_in, final_in)

    loss_value, pullback = jax.vjp(head_loss, first, inner_weight, outer_weight, final_weight)
    return pullback(jnp.ones((), F32))


def on_device(
    tokens,
    obs_mask,
    norm_gains,
    attn_in,
    attn_out,
    mlp_in,
    mlp_out,
    embodiment,
    levels,
    actions,
    noise,
    action_dims,
    head_read,
    head_act,
    time_table,
    block_in,
    block_out,
    head_out,
):
    width = attn_in.shape[3]
    heads = width // HDIM
    peers = lax.axis_size(DP)
    my_model = lax.axis_index("mp")
    my_owner = lax.axis_index(DP)
    owners = embodiment[:, 0]
    place = (jnp.arange(peers)[:, None] == owners[None, :]).astype(BF16)
    noisy = noisy_pair(levels, actions, noise, plan())
    marks = (levels + 1).astype(BF16)[..., None]
    early = jnp.concatenate([noisy, noise, marks, jnp.zeros((*levels.shape, 15), BF16)], axis=-1)
    sent = jnp.einsum("es,srf->erf", place, early, preferred_element_type=F32).astype(BF16)
    got = lax.all_to_all(sent, DP, split_axis=0, concat_axis=0, tiled=True)
    got = got.reshape(peers * READ, 128)

    def weights_of(layer):
        return gather_turned(
            (attn_in[layer], attn_out[layer], mlp_in[layer], mlp_out[layer]), DP, (1, 1, 0, 1)
        )

    residual = tokens.astype(F32)
    normed = normalize(residual, norm_gains[0]).astype(BF16)
    gathered = gather_rows(normed, "mp")
    mask_group = gather_rows(obs_mask, "mp")
    samples = mask_group.shape[0]
    allowed = allowed_keys(mask_group)
    qkv_weight, out_weight, up_weight, down_weight = weights_of(0)
    projected = jnp.einsum("td,jdc->jtc", gathered, qkv_weight, preferred_element_type=F32)
    projected = projected.astype(BF16).reshape(3, samples, SEQ, heads, HDIM)
    context = attend(projected[0], projected[1], projected[2], allowed).reshape(-1, width)
    residual = residual + summed_on_arrival(mm(context, out_weight).astype(BF16), "mp")
    normed = normalize(residual, norm_gains[1]).astype(BF16)
    gathered = gather_rows(normed, "mp")
    hidden = jax.nn.gelu(mm(gathered, up_weight), approximate=True).astype(BF16)
    residual = residual + summed_on_arrival(mm(hidden, down_weight).astype(BF16), "mp")
    whole = gather_rows(residual.astype(BF16), "mp").astype(F32)
    qkv_weight, out_weight, up_weight, down_weight = weights_of(1)
    normed = normalize(whole, norm_gains[2]).astype(BF16)
    last = slice(SEQ - READ, SEQ)
    ending = whole.reshape(samples, SEQ, D)[:, last].reshape(-1, D)
    normed_end = normed.reshape(samples, SEQ, D)[:, last].reshape(-1, D)
    queries = mm(normed_end, qkv_weight[0]).astype(BF16).reshape(samples, READ, heads, HDIM)
    key_rows = mm(normed, qkv_weight[1]).astype(BF16).reshape(samples, SEQ, heads, HDIM)
    value_rows = mm(normed, qkv_weight[2]).astype(BF16).reshape(samples, SEQ, heads, HDIM)
    context = attend(queries, key_rows, value_rows, allowed[:, last]).reshape(-1, width)
    ending = ending + summed_for_all(mm(context, out_weight).astype(BF16), "mp")
    normed = normalize(ending, norm_gains[3]).astype(BF16)
    hidden = jax.nn.gelu(mm(normed, up_weight), approximate=True).astype(BF16)
    ending = ending + summed_for_all(mm(hidden, down_weight).astype(BF16), "mp")
    readouts = normalize(ending, norm_gains[4]).astype(BF16).reshape(samples, READ * D)
    send = mm(place, readouts).astype(BF16)
    features = lax.all_to_all(send, DP, split_axis=0, concat_axis=0, tiled=True)
    features = features.reshape(peers * READ, D)
    head_noisy = got[:, :ACT]
    head_target = got[:, ACT : 2 * ACT].astype(F32)
    head_level = got[:, 2 * ACT].astype(jnp.int32) - 1
    onehot = (head_level[:, None] == jnp.arange(LEVELS)).astype(BF16)
    dims_here = jnp.sum(jnp.where(jnp.arange(EMB) == my_owner, action_dims, 0))
    column = jnp.arange(ACT) % ADIM_MAX
    weight_mask = (head_level >= 0).astype(F32)[:, None] * (column < dims_here).astype(F32)[None, :]
    others = mm(head_noisy, head_act[0]) + mm(onehot, time_table[0])
    first = mm(features, head_read[0]) + others
    grad_first, grad_inner, grad_outer, grad_final = head_grads(
        first,
        block_in[0].astype(F32),
        block_out[0].astype(F32),
        head_out[0].astype(F32),
        head_target,
        weight_mask,
    )
    grad_bf = grad_first.astype(BF16)
    backward = jnp.einsum("nc,dc->nd", grad_bf, head_read[0], preferred_element_type=F32)
    backward = backward.astype(BF16).reshape(peers, READ * D)
    arrived = lax.all_to_all(backward, DP, split_axis=0, concat_axis=0, tiled=True)
    mine = samples // 4
    own_place = lax.dynamic_slice_in_dim(place, my_model * mine, mine, 1)
    arrived = jnp.einsum("es,ef->sf", own_place, arrived, preferred_element_type=F32)
    arrived = arrived.astype(BF16).reshape(mine, READ, D)
    part = lax.dynamic_slice_in_dim(features, my_model * width, width, 1)
    grad_read = jnp.einsum("nd,nc->dc", part, grad_bf, preferred_element_type=F32)
    grad_act = jnp.einsum("na,nc->ac", head_noisy, grad_bf, preferred_element_type=F32)
    grad_time = jnp.einsum("nl,nc->lc", onehot, grad_bf, preferred_element_type=F32)
    return (
        arrived,
        grad_read[None],
        grad_act[None],
        grad_time[None],
        grad_inner[None],
        grad_outer[None],
        grad_final[None],
    )


def solution(mesh):
    fine = Mesh(mesh.devices.reshape(8, 4, 2, 4), ("z", "y", "c", "mp"))
    both = (*DP, "mp")
    placed = (
        P(both, None),
        P(both, None),
        P(),
        P(None, None, DP, "mp"),
        P(None, "mp", DP),
        P(None, DP, "mp"),
        P(None, "mp", DP),
        P(DP, None),
        P(DP, None),
        P(DP, None, None),
        P(DP, None, None),
        P(),
        P(DP, None, None),
        P(DP, None, None),
        P(DP, None, None),
        P(DP, None, None),
        P(DP, None, None),
        P(DP, None, None),
    )
    return jax.shard_map(
        on_device,
        mesh=fine,
        in_specs=placed,
        out_specs=(
            P(both, None, None),
            P(DP, "mp", None),
            P(DP, None, None),
            P(DP, None, None),
            P(DP, None, None),
            P(DP, None, None),
            P(DP, None, None),
        ),
        check_vma=False,
    )
```

profile of v0, /device:TPU:1, one launch (start us, length us, event | category | flops | bytes accessed | tf_op | source)
XLA Modules:
  0.0 302.3 jit_solution(15710188673894022588)
XLA Ops:
  12.4 4.8 %all-to-all-start.2 = ((s32[4,1,192]{2,1,0:T(1,128)}), s32[4,1,192]{2,1,0:T(1,128)S(1)}, u32[]{:S(2)}, u32[]{:S(2)}) async-start(s32[4,1,192]{2,1,0:T(1,128)} %reshape.374), calls=%async_computation.2 | async-start | bytes 8192 | tf_op jit(solution)/shard_map/all_to_all | solution.py:23
  18.8 2.6 all-to-all-done.2
  22.5 3.5 %all-to-all-start.1 = ((bf16[4,192,768]{2,1,0:T(8,128)(2,1)}), bf16[4,192,768]{2,1,0:T(8,128)(2,1)S(1)}, u32[]{:S(2)}, u32[]{:S(2)}) async-start(bf16[4,192,768]{2,1,0:T(8,128)(2,1)} %broadcast_in_dim.107), calls=%async_computation.1 | async-start | bytes 2359296 | tf_op jit(solution)/shard_map/all_to_all | solution.py:23
  27.6 67.6 %all-gather.5.cloned.1.call-done = bf16[64,12,2304]{2,1,0:T(8,128)(2,1)} async-done(((bf16[1,12,2304]{2,1,0:T(8,128)(2,1)}), bf16[64,12,2304]{2,1,0:T(8,128)(2,1)}) %all-gather.5.cloned.1.call-update) | async-done | bytes 3538960 | tf_op jit(solution)/shard_map/all_gather | solution.py:45
  95.2 6.4 %reshape.361 = bf16[768,2304]{1,0:T(8,128)(2,1)} reshape(bf16[64,12,2304]{2,1,0:T(8,128)(2,1)} %all-gather.5.cloned.1.call-done) | data formatting | bytes 7077888
  108.5 2.6 fusion.10
  115.9 19.9 %all_to_all.67 = bf16[4,192,768]{2,1,0:T(8,128)(2,1)S(1)} all-to-all(bf16[4,192,768]{2,1,0:T(8,128)(2,1)S(1)} %bitcast.164), channel_id=1, replica_groups=mesh['z'=8,'y'=4,'c'=2,'mp'=4] {'mp'}, dimensions={0} | all-to-all | bytes 2359296 | tf_op jit(solution)/shard_map/all_to_all | solution.py:33
  136.6 17.3 %all_to_all.68 = bf16[4,192,768]{2,1,0:T(8,128)(2,1)S(1)} all-to-all(bf16[4,192,768]{2,1,0:T(8,128)(2,1)S(1)} %broadcast_in_dim.111), channel_id=1, replica_groups=mesh['z'=8,'y'=4,'c'=2,'mp'=4] {'mp'}, dimensions={0} | all-to-all | bytes 2359296 | tf_op jit(solution)/shard_map/all_to_all | solution.py:23
  153.9 4.9 %convolution_convert_fusion.2 = bf16[768,768]{1,0:T(8,128)(2,1)} fusion(bf16[768,2304]{1,0:T(8,128)(2,1)} %reshape.361, bf16[768,768]{1,0:T(8,128)(2,1)S(1)} %bitcast.177), kind=kOutput, calls=%fused_computation.17 | convolution fusion | flops 1817837568 | bytes 4718592 | tf_op jit(solution)/shard_map/dot_general | solution.py:62
  158.8 3.7 %all-to-all-start.5 = ((bf16[4,192,768]{2,1,0:T(8,128)(2,1)}), bf16[4,192,768]{2,1,0:T(8,128)(2,1)S(1)}, u32[]{:S(2)}, u32[]{:S(2)}) async-start(bf16[4,192,768]{2,1,0:T(8,128)(2,1)} %bitcast.174), calls=%async_computation.5 | async-start | bytes 2359296 | tf_op jit(solution)/shard_map/all_to_all | solution.py:33
  162.9 13.6 %all-to-all-done.5 = bf16[4,192,768]{2,1,0:T(8,128)(2,1)S(1)} async-done(((bf16[4,192,768]{2,1,0:T(8,128)(2,1)}), bf16[4,192,768]{2,1,0:T(8,128)(2,1)S(1)}, u32[]{:S(2)}, u32[]{:S(2)}) %all-to-all-start.5) | async-done | bytes 1179680 | tf_op jit(solution)/shard_map/all_to_all | solution.py:33
  177.9 3.9 %all-to-all-start.6 = ((bf16[4,192,768]{2,1,0:T(8,128)(2,1)}), bf16[4,192,768]{2,1,0:T(8,128)(2,1)S(1)}, u32[]{:S(2)}, u32[]{:S(2)}) async-start(bf16[4,192,768]{2,1,0:T(8,128)(2,1)} %broadcast_in_dim.112), calls=%async_computation.6 | async-start | bytes 2359296 | tf_op jit(solution)/shard_map/all_to_all | solution.py:23
  184.7 6.4 %reshape.363 = bf16[768,2304]{1,0:T(8,128)(2,1)} reshape(bf16[64,12,2304]{2,1,0:T(8,128)(2,1)} %all-gather.7.cloned.1.call-done) | data formatting | bytes 7077888
  208.5 3.3 %all-to-all-start.7 = ((bf16[4,24,768]{2,1,0:T(8,128)(2,1)}), bf16[4,24,768]{2,1,0:T(8,128)(2,1)S(1)}, u32[]{:S(2)}, u32[]{:S(2)}) async-start(bf16[4,24,768]{2,1,0:T(8,128)(2,1)} %broadcast_in_dim.115), calls=%async_computation.7 | async-start | bytes 294912 | tf_op jit(solution)/shard_map/all_to_all | solution.py:23
  212.6 4.1 %all-to-all-done.7 = bf16[4,24,768]{2,1,0:T(8,128)(2,1)S(1)} async-done(((bf16[4,24,768]{2,1,0:T(8,128)(2,1)}), bf16[4,24,768]{2,1,0:T(8,128)(2,1)S(1)}, u32[]{:S(2)}, u32[]{:S(2)}) %all-to-all-start.7) | async-done | bytes 147488 | tf_op jit(solution)/shard_map/all_to_all | solution.py:23
  216.7 11.9 %all-to-all-start = ((bf16[64,2,128]{2,1,0:T(2,128)(2,1)}), bf16[64,2,128]{2,1,0:T(2,128)(2,1)S(1)}, u32[]{:S(2)}, u32[]{:S(2)}) async-start(bf16[64,2,128]{2,1,0:T(2,128)(2,1)} %copy.209), calls=%async_computation | async-start | bytes 65536 | tf_op jit(solution)/shard_map/all_to_all | solution.py:147
  231.1 2.4 fusion.32
  233.4 4.5 %all-to-all-done = bf16[64,2,128]{2,1,0:T(2,128)(2,1)S(1)} async-done(((bf16[64,2,128]{2,1,0:T(2,128)(2,1)}), bf16[64,2,128]{2,1,0:T(2,128)(2,1)S(1)}, u32[]{:S(2)}, u32[]{:S(2)}) %all-to-all-start) | async-done | bytes 32800 | tf_op jit(solution)/shard_map/all_to_all | solution.py:147
  238.6 3.3 %all-to-all-start.8 = ((bf16[4,24,768]{2,1,0:T(8,128)(2,1)}), bf16[4,24,768]{2,1,0:T(8,128)(2,1)S(1)}, u32[]{:S(2)}, u32[]{:S(2)}) async-start(bf16[4,24,768]{2,1,0:T(8,128)(2,1)} %broadcast_in_dim.116), calls=%async_computation.8 | async-start | bytes 294912 | tf_op jit(solution)/shard_map/all_to_all | solution.py:23
  242.2 4.6 %all-to-all-done.8 = bf16[4,24,768]{2,1,0:T(8,128)(2,1)S(1)} async-done(((bf16[4,24,768]{2,1,0:T(8,128)(2,1)}), bf16[4,24,768]{2,1,0:T(8,128)(2,1)S(1)}, u32[]{:S(2)}, u32[]{:S(2)}) %all-to-all-start.8) | async-done | bytes 147488 | tf_op jit(solution)/shard_map/all_to_all | solution.py:23
  250.8 7.0 %all-to-all-start.9 = ((bf16[64,2,768]{2,1,0:T(2,128)(2,1)}), bf16[64,2,768]{2,1,0:T(2,128)(2,1)S(1)}, u32[]{:S(2)}, u32[]{:S(2)}) async-start(bf16[64,2,768]{2,1,0:T(2,128)(2,1)} %reshape.376), calls=%async_computation.9 | async-start | bytes 393216 | tf_op jit(solution)/shard_map/all_to_all | solution.py:186
  258.7 11.2 %all-to-all-done.9 = bf16[64,2,768]{2,1,0:T(2,128)(2,1)S(1)} async-done(((bf16[64,2,768]{2,1,0:T(2,128)(2,1)}), bf16[64,2,768]{2,1,0:T(2,128)(2,1)S(1)}, u32[]{:S(2)}, u32[]{:S(2)}) %all-to-all-start.9) | async-done | bytes 196640 | tf_op jit(solution)/shard_map/all_to_all | solution.py:186
  277.2 4.5 %all-to-all-start.10 = ((bf16[64,2,768]{2,1,0:T(2,128)(2,1)}), bf16[64,2,768]{2,1,0:T(2,128)(2,1)S(1)}, u32[]{:S(2)}, u32[]{:S(2)}) async-start(bf16[64,2,768]{2,1,0:T(2,128)(2,1)} %reshape.378), calls=%async_computation.10 | async-start | bytes 393216 | tf_op jit(solution)/shard_map/all_to_all | solution.py:208
  285.7 8.1 %all-to-all-done.10 = bf16[64,2,768]{2,1,0:T(2,128)(2,1)S(1)} async-done(((bf16[64,2,768]{2,1,0:T(2,128)(2,1)}), bf16[64,2,768]{2,1,0:T(2,128)(2,1)S(1)}, u32[]{:S(2)}, u32[]{:S(2)}) %all-to-all-start.10) | async-done | bytes 196640 | tf_op jit(solution)/shard_map/all_to_all | solution.py:208
  (201 shorter events, 65.2 us)
Async XLA Ops:
  7.2 264.1 %copy-start = (bf16[1,768,256]{2,1,0:T(8,128)(2,1)S(1)}, bf16[1,768,256]{2,1,0:T(8,128)(2,1)}, u32[]{:S(2)}) copy-start(bf16[1,768,256]{2,1,0:T(8,128)(2,1)} %param.30) | copy-start | bytes 1179652
  7.2 4.6 %copy-start.10 = (s32[3,64]{1,0:T(4,128)S(1)}, s32[3,64]{1,0:T(4,128)}, u32[]{:S(2)}) copy-start(s32[3,64]{1,0:T(4,128)} %param.19) | copy-start | bytes 2308
  7.2 10.9 %copy-start.1 = (bf16[192,768]{1,0:T(8,128)(2,1)S(1)}, bf16[192,768]{1,0:T(8,128)(2,1)}, u32[]{:S(2)}) copy-start(bf16[192,768]{1,0:T(8,128)(2,1)} %param.18) | copy-start | bytes 884740
  7.2 11.3 %copy-start.6 = (f32[5,768]{1,0:T(8,128)S(1)}, f32[5,768]{1,0:T(8,128)}, u32[]{:S(2)}) copy-start(f32[5,768]{1,0:T(8,128)} %param.20) | copy-start | bytes 46084
  7.2 88.0 %all-gather.5.cloned.1.call-start = ((), (), s32[]{:S(2)}) async-start(), calls=%async_computation.11 | async-start | bytes 4792320 | tf_op jit(solution)/shard_map/all_gather | solution.py:45
  12.4 9.0 %all-to-all-start.2 = ((s32[4,1,192]{2,1,0:T(1,128)}), s32[4,1,192]{2,1,0:T(1,128)S(1)}, u32[]{:S(2)}, u32[]{:S(2)}) async-start(s32[4,1,192]{2,1,0:T(1,128)} %reshape.374), calls=%async_computation.2 | async-start | bytes 8192 | tf_op jit(solution)/shard_map/all_to_all | solution.py:23
  17.3 167.5 %all-gather.7.cloned.1.call-start = ((), (), s32[]{:S(2)}) async-start(), calls=%async_computation.12 | async-start | bytes 4792320 | tf_op jit(solution)/shard_map/all_gather | solution.py:45
  22.5 81.6 %all-to-all-start.1 = ((bf16[4,192,768]{2,1,0:T(8,128)(2,1)}), bf16[4,192,768]{2,1,0:T(8,128)(2,1)S(1)}, u32[]{:S(2)}, u32[]{:S(2)}) async-start(bf16[4,192,768]{2,1,0:T(8,128)(2,1)} %broadcast_in_dim.107), calls=%async_computation.1 | async-start | bytes 2359296 | tf_op jit(solution)/shard_map/all_to_all | solution.py:23
  158.8 3.7 %copy-start.11 = (s32[12,2]{0,1:T(2,128)S(1)}, s32[12,2]{0,1:T(2,128)}, u32[]{:S(2)}) copy-start(s32[12,2]{0,1:T(2,128)} %param.26) | copy-start | bytes 292
  158.8 17.7 %all-to-all-start.5 = ((bf16[4,192,768]{2,1,0:T(8,128)(2,1)}), bf16[4,192,768]{2,1,0:T(8,128)(2,1)S(1)}, u32[]{:S(2)}, u32[]{:S(2)}) async-start(bf16[4,192,768]{2,1,0:T(8,128)(2,1)} %bitcast.174), calls=%async_computation.5 | async-start | bytes 2359296 | tf_op jit(solution)/shard_map/all_to_all | solution.py:33
  177.9 4.0 %copy-start.4 = (bf16[12,2,56]{2,1,0:T(2,128)(2,1)S(1)}, bf16[12,2,56]{2,1,0:T(2,128)(2,1)}, u32[]{:S(2)}) copy-start(bf16[12,2,56]{2,1,0:T(2,128)(2,1)} %param.28) | copy-start | bytes 8068
  177.9 4.1 %copy-start.7 = (bf16[12,2,56]{2,1,0:T(2,128)(2,1)S(1)}, bf16[12,2,56]{2,1,0:T(2,128)(2,1)}, u32[]{:S(2)}) copy-start(bf16[12,2,56]{2,1,0:T(2,128)(2,1)} %param.27) | copy-start | bytes 8068
  177.9 4.2 %copy-start.8 = (s32[12,1]{0,1:T(1,128)S(1)}, s32[12,1]{0,1:T(1,128)}, u32[]{:S(2)}) copy-start(s32[12,1]{0,1:T(1,128)} %param.25) | copy-start | bytes 148
  177.9 5.1 %copy-start.15 = (s32[25]{0:T(128)S(1)}, s32[25]{0:T(128)}, u32[]{:S(2)}) copy-start(s32[25]{0:T(128)} %param.29) | copy-start | bytes 304
  177.9 16.5 %all-to-all-start.6 = ((bf16[4,192,768]{2,1,0:T(8,128)(2,1)}), bf16[4,192,768]{2,1,0:T(8,128)(2,1)S(1)}, u32[]{:S(2)}, u32[]{:S(2)}) async-start(bf16[4,192,768]{2,1,0:T(8,128)(2,1)} %broadcast_in_dim.112), calls=%async_computation.6 | async-start | bytes 2359296 | tf_op jit(solution)/shard_map/all_to_all | solution.py:23
  208.5 8.2 %all-to-all-start.7 = ((bf16[4,24,768]{2,1,0:T(8,128)(2,1)}), bf16[4,24,768]{2,1,0:T(8,128)(2,1)S(1)}, u32[]{:S(2)}, u32[]{:S(2)}) async-start(bf16[4,24,768]{2,1,0:T(8,128)(2,1)} %broadcast_in_dim.115), calls=%async_computation.7 | async-start | bytes 294912 | tf_op jit(solution)/shard_map/all_to_all | solution.py:23
  216.7 21.2 %all-to-all-start = ((bf16[64,2,128]{2,1,0:T(2,128)(2,1)}), bf16[64,2,128]{2,1,0:T(2,128)(2,1)S(1)}, u32[]{:S(2)}, u32[]{:S(2)}) async-start(bf16[64,2,128]{2,1,0:T(2,128)(2,1)} %copy.209), calls=%async_computation | async-start | bytes 65536 | tf_op jit(solution)/shard_map/all_to_all | solution.py:147
  231.1 10.8 %copy-start.3 = (bf16[1,56,256]{2,1,0:T(8,128)(2,1)S(1)}, bf16[1,56,256]{2,1,0:T(8,128)(2,1)}, u32[]{:S(2)}) copy-start(bf16[1,56,256]{2,1,0:T(8,128)(2,1)} %param.31) | copy-start | bytes 86020
  238.6 8.2 %all-to-all-start.8 = ((bf16[4,24,768]{2,1,0:T(8,128)(2,1)}), bf16[4,24,768]{2,1,0:T(8,128)(2,1)S(1)}, u32[]{:S(2)}, u32[]{:S(2)}) async-start(bf16[4,24,768]{2,1,0:T(8,128)(2,1)} %broadcast_in_dim.116), calls=%async_computation.8 | async-start | bytes 294912 | tf_op jit(solution)/shard_map/all_to_all | solution.py:23
  242.1 6.5 %copy-start.9 = (s32[12,1]{0,1:T(1,128)S(1)}, s32[12,1]{0,1:T(1,128)}, u32[]{:S(2)}) copy-start(s32[12,1]{0,1:T(1,128)} %param.25) | copy-start | bytes 148
  248.5 10.0 %copy-start.5 = (bf16[1,20,256]{2,1,0:T(8,128)(2,1)S(1)}, bf16[1,20,256]{2,1,0:T(8,128)(2,1)}, u32[]{:S(2)}) copy-start(bf16[1,20,256]{2,1,0:T(8,128)(2,1)} %param.32) | copy-start | bytes 30724
  250.8 19.0 %all-to-all-start.9 = ((bf16[64,2,768]{2,1,0:T(2,128)(2,1)}), bf16[64,2,768]{2,1,0:T(2,128)(2,1)S(1)}, u32[]{:S(2)}, u32[]{:S(2)}) async-start(bf16[64,2,768]{2,1,0:T(2,128)(2,1)} %reshape.376), calls=%async_computation.9 | async-start | bytes 393216 | tf_op jit(solution)/shard_map/all_to_all | solution.py:186
  258.7 12.8 %copy-start.13 = (bf16[1,256,256]{2,1,0:T(8,128)(2,1)S(1)}, bf16[1,256,256]{2,1,0:T(8,128)(2,1)}, u32[]{:S(2)}) copy-start(bf16[1,256,256]{2,1,0:T(8,128)(2,1)} %param.33) | copy-start | bytes 393220
  277.2 16.6 %all-to-all-start.10 = ((bf16[64,2,768]{2,1,0:T(2,128)(2,1)}), bf16[64,2,768]{2,1,0:T(2,128)(2,1)S(1)}, u32[]{:S(2)}, u32[]{:S(2)}) async-start(bf16[64,2,768]{2,1,0:T(2,128)(2,1)} %reshape.378), calls=%async_computation.10 | async-start | bytes 393216 | tf_op jit(solution)/shard_map/all_to_all | solution.py:208
  (5 other events, 6.2 us)
Sparse Core Ops, SparseCore 0:
  11.9 83.2 all-gather.4
  98.5 76.5 all-gather.6
where the time goes:
time: 304 us; the launch traced here: 302 us
  waiting for transfers between devices  118 us (39%)
  starting transfers between devices  45.9 us (15%)
  local copies, waits for them, and re-layouts  42.7 us (14%)
  blocking collectives  37.2 us (12%)
  matrix products  29.9 us (10%)
  between operations  14.9 us (5%)
  other arithmetic  13.7 us (5%)
    all_gather x2, waiting for transfers between devices, gather_turned(): whole = lax.all_gather(both, axis, axis=0, tiled=True)  67.6 us
    all_to_all x1, blocking collectives, summed_on_arrival(): lax.all_to_all(pieces, axis, split_axis=0, concat_axis=0, tiled=True)  19.9 us
    all_to_all x5, starting transfers between devices, sent_to_all(): return lax.all_to_all(copies, axis, split_axis=0, concat_axis=0, tiled=True)  18.9 us
    unnamed x50, local copies, waits for them, and re-layouts  18.1 us
    all_to_all x1, blocking collectives, sent_to_all(): return lax.all_to_all(copies, axis, split_axis=0, concat_axis=0, tiled=True)  17.3 us
    dot_general x11, matrix products, mm(): return jnp.dot(a, b, preferred_element_type=F32)  14 us
    all_to_all x1, waiting for transfers between devices, summed_on_arrival(): lax.all_to_all(pieces, axis, split_axis=0, concat_axis=0, tiled=True)  13.6 us
    all_to_all x5, waiting for transfers between devices, sent_to_all(): return lax.all_to_all(copies, axis, split_axis=0, concat_axis=0, tiled=True)  12.9 us
  transfers between devices with their start and end apart: 11, of which 9 were waited for; matrix products, arithmetic and copies ran while one was open for 17% of the time, Pallas kernels for 0%

commit v1 on v0

--- a/solution.py
+++ b/solution.py
@@ -42,7 +42,9 @@
     turned = [jnp.moveaxis(a, dim, 0) for a, dim in zip(arrays, dims)]
     widths = [t[0].size for t in turned]
     both = jnp.concatenate([t.reshape(-1, w) for t, w in zip(turned, widths)], axis=1)
-    whole = lax.all_gather(both, axis, axis=0, tiled=True)
+    whole = jnp.concatenate(
+        lax.all_to_all(jnp.stack([both] * lax.axis_size(axis)), axis, 0, 0), axis=0
+    )
     pieces = jnp.split(whole, [sum(widths[:k]) for k in range(1, len(widths))], axis=1)
     return tuple(
         (

time: 304 us -> 462 us (1.52)
  waiting for transfers between devices: 118 us -> 259 us
  starting transfers between devices: 45.9 us -> 81.2 us
  between operations: 14.9 us -> 1.47 us
  blocking collectives: 37.2 us -> 29.4 us
  local copies, waits for them, and re-layouts: 42.7 us -> 48.6 us
    all_to_all x0 -> x2, waiting for transfers between devices: none -> 209 us  [gather_turned(): lax.all_to_all(jnp.stack([both] * lax.axis_size(axis)), axis, 0, 0)]
    all_gather x2 -> x0, waiting for transfers between devices: 67.6 us -> none  [gather_turned(): whole = lax.all_gather(both, axis, axis=0, tiled=True)]
    all_to_all x0 -> x2, starting transfers between devices: none -> 35.8 us  [gather_turned(): lax.all_to_all(jnp.stack([both] * lax.axis_size(axis)), axis, 0, 0)]
    unnamed x50 -> x58, local copies, waits for them, and re-layouts: 18.1 us -> 5.14 us
    reshape x0 -> x2, local copies, waits for them, and re-layouts: none -> 12.8 us  [gather_turned(): jnp.concatenate(lax.all_to_all(jnp.stack([both] * lax.axis_size(axis)), a...]
    another operation x0 -> x2, local copies, waits for them, and re-layouts: none -> 4.95 us  [gather_turned(): jnp.stack([both] * lax.axis_size(axis))]
    all_to_all x1, blocking collectives: 19.9 us -> 15.1 us  [summed_on_arrival(): lax.all_to_all(pieces, axis, split_axis=0, concat_axis=0, tiled=True)]
  transfers between devices with their start and end apart: 11 -> 11, of which waited for: 9 -> 10; matrix products, arithmetic and copies ran while one was open for 17% -> 8% of each run, Pallas kernels for 0% -> 0%
where the time goes in v1:
time: 462 us; the launch traced here: 460 us
  waiting for transfers between devices  259 us (56%)
  starting transfers between devices  81.2 us (18%)
  local copies, waits for them, and re-layouts  48.6 us (11%)
  blocking collectives  29.4 us (6%)
  matrix products  26.8 us (6%)
  other arithmetic  13.2 us (3%)
    all_to_all x2, waiting for transfers between devices, gather_turned(): lax.all_to_all(jnp.stack([both] * lax.axis_size(axis)), axis, 0, 0)  209 us
    all_to_all x2, starting transfers between devices, gather_turned(): lax.all_to_all(jnp.stack([both] * lax.axis_size(axis)), axis, 0, 0)  35.8 us
    all_to_all x5, starting transfers between devices, sent_to_all(): return lax.all_to_all(copies, axis, split_axis=0, concat_axis=0, tiled=True)  19.7 us
    all_to_all x5, waiting for transfers between devices, sent_to_all(): return lax.all_to_all(copies, axis, split_axis=0, concat_axis=0, tiled=True)  15.7 us
    all_to_all x1, blocking collectives, summed_on_arrival(): lax.all_to_all(pieces, axis, split_axis=0, concat_axis=0, tiled=True)  15.1 us
    all_to_all x1, blocking collectives, sent_to_all(): return lax.all_to_all(copies, axis, split_axis=0, concat_axis=0, tiled=True)  14.3 us
    dot_general x11, matrix products, mm(): return jnp.dot(a, b, preferred_element_type=F32)  13.9 us
    reshape x2, local copies, waits for them, and re-layouts, gather_turned(): jnp.concatenate(lax.all_to_all(jnp.stack([both] * lax.axis_size(axis)), a...  12.8 us
  transfers between devices with their start and end apart: 11, of which 10 were waited for; matrix products, arithmetic and copies ran while one was open for 8% of the time, Pallas kernels for 0%

profile of v1, /device:TPU:1, one launch (start us, length us, event | category | flops | bytes accessed | tf_op | source)
XLA Modules:
  0.0 460.0 jit_solution(14792417717089599267)
XLA Ops:
  2.1 4.8 %all-to-all-start.3 = ((s32[4,1,192]{2,1,0:T(1,128)}), s32[4,1,192]{2,1,0:T(1,128)S(1)}, u32[]{:S(2)}, u32[]{:S(2)}) async-start(s32[4,1,192]{2,1,0:T(1,128)} %reshape.382), calls=%async_computation.3 | async-start | bytes 8192 | tf_op jit(solution)/shard_map/all_to_all | solution.py:23
  15.0 12.9 %all-to-all-start.1 = ((bf16[64,12,2304]{2,1,0:T(8,128)(2,1)}), bf16[64,12,2304]{2,1,0:T(8,128)(2,1)}, u32[]{:S(2)}, u32[]{:S(2)}) async-start(bf16[64,12,2304]{2,1,0:T(8,128)(2,1)} %stack.4), calls=%async_computation.1 | async-start | bytes 9437184 | tf_op jit(solution)/shard_map/all_to_all | solution.py:46
  29.1 104.4 %all-to-all-done.1 = bf16[64,12,2304]{2,1,0:T(8,128)(2,1)} async-done(((bf16[64,12,2304]{2,1,0:T(8,128)(2,1)}), bf16[64,12,2304]{2,1,0:T(8,128)(2,1)}, u32[]{:S(2)}, u32[]{:S(2)}) %all-to-all-start.1) | async-done | bytes 3538976 | tf_op jit(solution)/shard_map/all_to_all | solution.py:46
  134.7 4.5 all-to-all-start.2
  140.7 6.4 %reshape.351 = bf16[768,2304]{1,0:T(8,128)(2,1)} reshape(bf16[64,12,2304]{2,1,0:T(8,128)(2,1)} %all-to-all-done.1) | data formatting | bytes 7077888 | tf_op jit(solution)/shard_map/reshape | solution.py:45
  163.4 15.1 %all_to_all.77 = bf16[4,192,768]{2,1,0:T(8,128)(2,1)S(1)} all-to-all(bf16[4,192,768]{2,1,0:T(8,128)(2,1)S(1)} %bitcast.162), channel_id=1, replica_groups=mesh['z'=8,'y'=4,'c'=2,'mp'=4] {'mp'}, dimensions={0} | all-to-all | bytes 2359296 | tf_op jit(solution)/shard_map/all_to_all | solution.py:33
  179.3 14.3 %all_to_all.78 = bf16[4,192,768]{2,1,0:T(8,128)(2,1)S(1)} all-to-all(bf16[4,192,768]{2,1,0:T(8,128)(2,1)S(1)} %broadcast_in_dim.111), channel_id=1, replica_groups=mesh['z'=8,'y'=4,'c'=2,'mp'=4] {'mp'}, dimensions={0} | all-to-all | bytes 2359296 | tf_op jit(solution)/shard_map/all_to_all | solution.py:23
  193.6 4.8 %convolution_convert_fusion.2 = bf16[768,768]{1,0:T(8,128)(2,1)} fusion(bf16[768,2304]{1,0:T(8,128)(2,1)} %reshape.351, bf16[768,768]{1,0:T(8,128)(2,1)S(1)} %bitcast.175), kind=kOutput, calls=%fused_computation.17 | convolution fusion | flops 1817837568 | bytes 4718592 | tf_op jit(solution)/shard_map/dot_general | solution.py:64
  198.4 3.7 all-to-all-start.6
  202.3 10.5 %all-to-all-done.6 = bf16[4,192,768]{2,1,0:T(8,128)(2,1)S(1)} async-done(((bf16[4,192,768]{2,1,0:T(8,128)(2,1)}), bf16[4,192,768]{2,1,0:T(8,128)(2,1)S(1)}, u32[]{:S(2)}, u32[]{:S(2)}) %all-to-all-start.6) | async-done | bytes 1179680 | tf_op jit(solution)/shard_map/all_to_all | solution.py:33
  215.2 22.9 %all-to-all-start.8 = ((bf16[64,12,2304]{2,1,0:T(8,128)(2,1)}), bf16[64,12,2304]{2,1,0:T(8,128)(2,1)}, u32[]{:S(2)}, u32[]{:S(2)}) async-start(bf16[64,12,2304]{2,1,0:T(8,128)(2,1)} %stack.5), calls=%async_computation.8 | async-start | bytes 9437184 | tf_op jit(solution)/shard_map/all_to_all | solution.py:46
  238.8 105.1 %all-to-all-done.8 = bf16[64,12,2304]{2,1,0:T(8,128)(2,1)} async-done(((bf16[64,12,2304]{2,1,0:T(8,128)(2,1)}), bf16[64,12,2304]{2,1,0:T(8,128)(2,1)}, u32[]{:S(2)}, u32[]{:S(2)}) %all-to-all-start.8) | async-done | bytes 3538976 | tf_op jit(solution)/shard_map/all_to_all | solution.py:46
  345.1 3.7 all-to-all-start.7
  351.2 6.4 %reshape.360 = bf16[768,2304]{1,0:T(8,128)(2,1)} reshape(bf16[64,12,2304]{2,1,0:T(8,128)(2,1)} %all-to-all-done.8) | data formatting | bytes 7077888 | tf_op jit(solution)/shard_map/reshape | solution.py:45
  359.4 3.7 all-to-all-done.7
  375.0 3.3 all-to-all-start.9
  379.1 4.1 all-to-all-done.9
  383.2 10.6 %all-to-all-start = ((bf16[64,2,128]{2,1,0:T(2,128)(2,1)}), bf16[64,2,128]{2,1,0:T(2,128)(2,1)S(1)}, u32[]{:S(2)}, u32[]{:S(2)}) async-start(bf16[64,2,128]{2,1,0:T(2,128)(2,1)} %copy.209), calls=%async_computation | async-start | bytes 65536 | tf_op jit(solution)/shard_map/all_to_all | solution.py:149
  398.7 4.5 all-to-all-done
  407.4 4.6 %all-to-all-done.10 = bf16[4,24,768]{2,1,0:T(8,128)(2,1)S(1)} async-done(((bf16[4,24,768]{2,1,0:T(8,128)(2,1)}), bf16[4,24,768]{2,1,0:T(8,128)(2,1)S(1)}, u32[]{:S(2)}, u32[]{:S(2)}) %all-to-all-start.10) | async-done | bytes 147488 | tf_op jit(solution)/shard_map/all_to_all | solution.py:23
  416.1 7.0 %all-to-all-start.11 = ((bf16[64,2,768]{2,1,0:T(2,128)(2,1)}), bf16[64,2,768]{2,1,0:T(2,128)(2,1)S(1)}, u32[]{:S(2)}, u32[]{:S(2)}) async-start(bf16[64,2,768]{2,1,0:T(2,128)(2,1)} %reshape.384), calls=%async_computation.11 | async-start | bytes 393216 | tf_op jit(solution)/shard_map/all_to_all | solution.py:188
  423.9 11.2 %all-to-all-done.11 = bf16[64,2,768]{2,1,0:T(2,128)(2,1)S(1)} async-done(((bf16[64,2,768]{2,1,0:T(2,128)(2,1)}), bf16[64,2,768]{2,1,0:T(2,128)(2,1)S(1)}, u32[]{:S(2)}, u32[]{:S(2)}) %all-to-all-start.11) | async-done | bytes 196640 | tf_op jit(solution)/shard_map/all_to_all | solution.py:188
  442.5 4.5 all-to-all-start.12
  451.0 8.1 %all-to-all-done.12 = bf16[64,2,768]{2,1,0:T(2,128)(2,1)S(1)} async-done(((bf16[64,2,768]{2,1,0:T(2,128)(2,1)}), bf16[64,2,768]{2,1,0:T(2,128)(2,1)S(1)}, u32[]{:S(2)}, u32[]{:S(2)}) %all-to-all-start.12) | async-done | bytes 196640 | tf_op jit(solution)/shard_map/all_to_all | solution.py:210
  (211 shorter events, 77.4 us)
Async XLA Ops:
  0.6 435.9 %copy-start = (bf16[1,768,256]{2,1,0:T(8,128)(2,1)S(1)}, bf16[1,768,256]{2,1,0:T(8,128)(2,1)}, u32[]{:S(2)}) copy-start(bf16[1,768,256]{2,1,0:T(8,128)(2,1)} %param.30) | copy-start | bytes 1179652
  2.1 10.4 %all-to-all-start.3 = ((s32[4,1,192]{2,1,0:T(1,128)}), s32[4,1,192]{2,1,0:T(1,128)S(1)}, u32[]{:S(2)}, u32[]{:S(2)}) async-start(s32[4,1,192]{2,1,0:T(1,128)} %reshape.382), calls=%async_computation.3 | async-start | bytes 8192 | tf_op jit(solution)/shard_map/all_to_all | solution.py:23
  15.0 12.9 %copy-start.11 = (f32[5,768]{1,0:T(8,128)S(1)}, f32[5,768]{1,0:T(8,128)}, u32[]{:S(2)}) copy-start(f32[5,768]{1,0:T(8,128)} %param.20) | copy-start | bytes 46084
  15.0 13.6 %copy-start.1 = (bf16[192,768]{1,0:T(8,128)(2,1)S(1)}, bf16[192,768]{1,0:T(8,128)(2,1)}, u32[]{:S(2)}) copy-start(bf16[192,768]{1,0:T(8,128)(2,1)} %param.18) | copy-start | bytes 884740
  15.0 118.5 %all-to-all-start.1 = ((bf16[64,12,2304]{2,1,0:T(8,128)(2,1)}), bf16[64,12,2304]{2,1,0:T(8,128)(2,1)}, u32[]{:S(2)}, u32[]{:S(2)}) async-start(bf16[64,12,2304]{2,1,0:T(8,128)(2,1)} %stack.4), calls=%async_computation.1 | async-start | bytes 9437184 | tf_op jit(solution)/shard_map/all_to_all | solution.py:46
  134.7 18.1 %all-to-all-start.2 = ((bf16[4,192,768]{2,1,0:T(8,128)(2,1)}), bf16[4,192,768]{2,1,0:T(8,128)(2,1)S(1)}, u32[]{:S(2)}, u32[]{:S(2)}) async-start(bf16[4,192,768]{2,1,0:T(8,128)(2,1)} %broadcast_in_dim.107), calls=%async_computation.2 | async-start | bytes 2359296 | tf_op jit(solution)/shard_map/all_to_all | solution.py:23
  198.4 14.3 %all-to-all-start.6 = ((bf16[4,192,768]{2,1,0:T(8,128)(2,1)}), bf16[4,192,768]{2,1,0:T(8,128)(2,1)S(1)}, u32[]{:S(2)}, u32[]{:S(2)}) async-start(bf16[4,192,768]{2,1,0:T(8,128)(2,1)} %bitcast.172), calls=%async_computation.6 | async-start | bytes 2359296 | tf_op jit(solution)/shard_map/all_to_all | solution.py:33
  215.2 22.9 %copy-start.16 = (s32[12,2]{0,1:T(2,128)S(1)}, s32[12,2]{0,1:T(2,128)}, u32[]{:S(2)}) copy-start(s32[12,2]{0,1:T(2,128)} %param.26) | copy-start | bytes 292
  215.2 128.7 %all-to-all-start.8 = ((bf16[64,12,2304]{2,1,0:T(8,128)(2,1)}), bf16[64,12,2304]{2,1,0:T(8,128)(2,1)}, u32[]{:S(2)}, u32[]{:S(2)}) async-start(bf16[64,12,2304]{2,1,0:T(8,128)(2,1)} %stack.5), calls=%async_computation.8 | async-start | bytes 9437184 | tf_op jit(solution)/shard_map/all_to_all | solution.py:46
  345.1 3.9 copy-start.8
  345.1 4.0 copy-start.12
  345.1 4.0 copy-start.14
  345.1 5.0 %copy-start.20 = (s32[25]{0:T(128)S(1)}, s32[25]{0:T(128)}, u32[]{:S(2)}) copy-start(s32[25]{0:T(128)} %param.29) | copy-start | bytes 304
  345.1 18.0 %all-to-all-start.7 = ((bf16[4,192,768]{2,1,0:T(8,128)(2,1)}), bf16[4,192,768]{2,1,0:T(8,128)(2,1)S(1)}, u32[]{:S(2)}, u32[]{:S(2)}) async-start(bf16[4,192,768]{2,1,0:T(8,128)(2,1)} %broadcast_in_dim.112), calls=%async_computation.7 | async-start | bytes 2359296 | tf_op jit(solution)/shard_map/all_to_all | solution.py:23
  372.8 23.5 %copy-start.13 = (f32[768]{0:T(1024)S(1)}, f32[768]{0:T(1024)}, u32[]{:S(2)}) copy-start(f32[768]{0:T(1024)} %get-tuple-element.60) | copy-start | bytes 9220
  375.0 8.2 %all-to-all-start.9 = ((bf16[4,24,768]{2,1,0:T(8,128)(2,1)}), bf16[4,24,768]{2,1,0:T(8,128)(2,1)S(1)}, u32[]{:S(2)}, u32[]{:S(2)}) async-start(bf16[4,24,768]{2,1,0:T(8,128)(2,1)} %broadcast_in_dim.115), calls=%async_computation.9 | async-start | bytes 294912 | tf_op jit(solution)/shard_map/all_to_all | solution.py:23
  383.2 19.9 %all-to-all-start = ((bf16[64,2,128]{2,1,0:T(2,128)(2,1)}), bf16[64,2,128]{2,1,0:T(2,128)(2,1)S(1)}, u32[]{:S(2)}, u32[]{:S(2)}) async-start(bf16[64,2,128]{2,1,0:T(2,128)(2,1)} %copy.209), calls=%async_computation | async-start | bytes 65536 | tf_op jit(solution)/shard_map/all_to_all | solution.py:149
  396.4 10.8 %copy-start.7 = (bf16[1,56,256]{2,1,0:T(8,128)(2,1)S(1)}, bf16[1,56,256]{2,1,0:T(8,128)(2,1)}, u32[]{:S(2)}) copy-start(bf16[1,56,256]{2,1,0:T(8,128)(2,1)} %param.31) | copy-start | bytes 86020
  403.8 8.2 %all-to-all-start.10 = ((bf16[4,24,768]{2,1,0:T(8,128)(2,1)}), bf16[4,24,768]{2,1,0:T(8,128)(2,1)S(1)}, u32[]{:S(2)}, u32[]{:S(2)}) async-start(bf16[4,24,768]{2,1,0:T(8,128)(2,1)} %broadcast_in_dim.116), calls=%async_computation.10 | async-start | bytes 294912 | tf_op jit(solution)/shard_map/all_to_all | solution.py:23
  407.3 6.5 %copy-start.15 = (s32[12,1]{0,1:T(1,128)S(1)}, s32[12,1]{0,1:T(1,128)}, u32[]{:S(2)}) copy-start(s32[12,1]{0,1:T(1,128)} %param.25) | copy-start | bytes 148
  413.7 10.0 %copy-start.10 = (bf16[1,20,256]{2,1,0:T(8,128)(2,1)S(1)}, bf16[1,20,256]{2,1,0:T(8,128)(2,1)}, u32[]{:S(2)}) copy-start(bf16[1,20,256]{2,1,0:T(8,128)(2,1)} %param.32) | copy-start | bytes 30724
  416.1 19.0 %all-to-all-start.11 = ((bf16[64,2,768]{2,1,0:T(2,128)(2,1)}), bf16[64,2,768]{2,1,0:T(2,128)(2,1)S(1)}, u32[]{:S(2)}, u32[]{:S(2)}) async-start(bf16[64,2,768]{2,1,0:T(2,128)(2,1)} %reshape.384), calls=%async_computation.11 | async-start | bytes 393216 | tf_op jit(solution)/shard_map/all_to_all | solution.py:188
  423.9 12.8 %copy-start.18 = (bf16[1,256,256]{2,1,0:T(8,128)(2,1)S(1)}, bf16[1,256,256]{2,1,0:T(8,128)(2,1)}, u32[]{:S(2)}) copy-start(bf16[1,256,256]{2,1,0:T(8,128)(2,1)} %param.33) | copy-start | bytes 393220
  442.5 16.6 %all-to-all-start.12 = ((bf16[64,2,768]{2,1,0:T(2,128)(2,1)}), bf16[64,2,768]{2,1,0:T(2,128)(2,1)S(1)}, u32[]{:S(2)}, u32[]{:S(2)}) async-start(bf16[64,2,768]{2,1,0:T(2,128)(2,1)} %reshape.386), calls=%async_computation.12 | async-start | bytes 393216 | tf_op jit(solution)/shard_map/all_to_all | solution.py:210
  (10 other events, 22.7 us)
